TPU v7x, 32 devices: a whole 2x2x4 slice. The times are simulated.
32 devices in a mesh: prow: 4 (over y, core), pcol: 8 (over z, x).
Axes of the slice: x: 2, y: 2, z: 4, core: 2. Of those that a mesh axis runs over, the one named last changes fastest.
Arguments:
- ainv_trail: float32 [2048, 2048], P('prow', 'pcol')
- panel_parent: float32 [2048, 256], P('prow', 'pcol'), may hold values from -0.125 to 0.125
- panel_child: float32 [2048, 256], P('prow', 'pcol'), may hold values from -0.125 to 0.125
- link_block: float32 [256, 256], replicated, may hold values from -0.375 to 0.375
- dinv_parent: float32 [256, 256], replicated
- dinv_child: float32 [256, 256], replicated
- pattern_parent: int32 [8], replicated, may hold values from 0 to 1, as said below
- pattern_child: int32 [8], replicated, may hold values from 0 to 1, as said below
Outputs:
- row_parent: float32 [256, 2048], P('prow', 'pcol')
- diag_parent: float32 [256, 256], P('prow')
- cross_child: float32 [256, 256], P('prow')
- row_child: float32 [256, 2048], P('prow', 'pcol')
- diag_child: float32 [256, 256], P('prow')
Inputs may be any that keep to these rules, and one draw needn't show every extreme that they name: `pattern_parent`: each entry is 0 or 1; the first entry is 1 and at least one entry is 0. `pattern_child`: each entry is 0 or 1, and is 1 only where pattern_parent is 1; the first entry is 1.
All inputs are finite; a program needn't handle non-finite values.
Results may differ from a plain program's by a relative error of at most 0.00009.
Values sent between devices are 32-bit elements; how exact they have to be, the bound alone decides.
A program may use at most 64 MiB of HBM per device.

v0:
```python
import jax
import jax.numpy as jnp
from jax import lax
from jax.sharding import PartitionSpec as P

highest = lax.Precision.HIGHEST


def lead_product(left, right):
    return lax.dot_general(
        left, right, (((0,), (0,)), ((), ())), precision=highest, preferred_element_type=jnp.float32
    )


def plain_product(left, right):
    return jnp.dot(left, right, precision=highest, preferred_element_type=jnp.float32)


def block_mask(pattern, first, count, width):
    picked = lax.dynamic_slice(pattern, (first,), (count,)).astype(jnp.float32)
    return jnp.repeat(picked, width)


def row_total(partial_value, columns, row_index, share):
    total = lax.psum(partial_value, "prow")
    whole = -total * columns[None, :]
    return (lax.dynamic_slice_in_dim(whole, row_index * share, share, 0), whole)


def total_terms(stacked):
    return lax.psum(stacked, ("prow", "pcol"))


def column_terms(row_part, blocks):
    result = plain_product(row_part, blocks[0])
    return result


def on_device(
    ainv_trail,
    panel_parent,
    panel_child,
    link_block,
    dinv_parent,
    dinv_child,
    pattern_parent,
    pattern_child,
):
    width = link_block.shape[0]
    row_count = lax.axis_size("prow")
    row_index = lax.axis_index("prow")
    col_index = lax.axis_index("pcol")
    row_blocks = ainv_trail.shape[0] // width
    col_blocks = ainv_trail.shape[1] // width
    share = width // row_count
    first_row = row_index * row_blocks
    first_col = col_index * col_blocks
    parent_whole, child_whole = (
        lax.all_gather(panel_parent, "pcol", axis=1, tiled=True),
        lax.all_gather(panel_child, "pcol", axis=1, tiled=True),
    )
    parent_rows = parent_whole * block_mask(pattern_parent, first_row, row_blocks, width)[:, None]
    child_rows = child_whole * block_mask(pattern_child, first_row, row_blocks, width)[:, None]
    parent_cols = block_mask(pattern_parent, first_col, col_blocks, width)
    child_cols = block_mask(pattern_child, first_col, col_blocks, width)
    parent_partial = lead_product(parent_rows, ainv_trail)
    child_partial = lead_product(child_rows, ainv_trail)
    link_share = lax.dynamic_slice_in_dim(link_block, row_index * share, share, 0)
    block = first_col + 0
    root = block // row_blocks
    local = jnp.clip(block - first_row, 0, row_blocks - 1)
    parent_piece = lax.dynamic_slice_in_dim(parent_rows, local * width, width, 0)
    child_piece = lax.dynamic_slice_in_dim(child_rows, local * width, width, 0)
    owner = (root == row_index).astype(jnp.float32)
    parent_piece = parent_piece * owner
    child_piece = child_piece * owner
    parent_blocks = [parent_piece]
    child_blocks = [child_piece]
    parent_share, parent_part = row_total(parent_partial, parent_cols, row_index, share)
    first_terms = total_terms(
        jnp.stack(
            [column_terms(parent_part, parent_blocks), column_terms(parent_part, child_blocks)]
        )
    )
    diag_parent = dinv_parent - first_terms[0]
    cross_child = -(lead_product(link_block, diag_parent) + first_terms[1].T)
    child_partial = child_partial + lead_product(link_share, parent_share)
    child_share, child_part = row_total(child_partial, child_cols, row_index, share)
    second_terms = total_terms(jnp.stack([column_terms(child_part, child_blocks)]))
    diag_child = dinv_child - plain_product(cross_child, link_block) - second_terms[0]
    start = row_index * share
    return (
        parent_share,
        lax.dynamic_slice_in_dim(diag_parent, start, share, 0),
        lax.dynamic_slice_in_dim(cross_child, start, share, 0),
        child_share,
        lax.dynamic_slice_in_dim(diag_child, start, share, 0),
    )


def solution(mesh):
    return jax.shard_map(
        on_device,
        mesh=mesh,
        in_specs=(P("prow", "pcol"), P("prow", "pcol"), P("prow", "pcol"), P(), P(), P(), P(), P()),
        out_specs=(
            P("prow", "pcol"),
            P("prow", None),
            P("prow", None),
            P("prow", "pcol"),
            P("prow", None),
        ),
        check_vma=False,
    )
```

profile of v0, /device:TPU:0, one launch (start us, length us, event | category | flops | bytes accessed | tf_op | source)
XLA Modules:
  0.0 260.4 jit_solution(992268018349741853)
XLA Ops:
  7.3 0.7 copy-done.6
  8.1 33.2 %all_gather.6 = f32[512,256]{0,1:T(8,128)S(1)} all-gather(f32[512,32]{0,1:T(8,128)} %param.9), channel_id=1, replica_groups=mesh['prow'=4,'pcol'=8] {'pcol'}, dimensions={1}, use_global_device_ids=true | all-gather | bytes 589824 | tf_op jit(solution)/shard_map/all_gather | solution.py:59
  41.4 1.3 fusion.13
  42.8 0.6 dynamic_slice.45
  43.4 0.6 dynamic_slice.37
  45.4 31.2 %all_gather.7 = f32[512,256]{0,1:T(8,128)S(1)} all-gather(f32[512,32]{0,1:T(8,128)S(1)} %copy-done.5), channel_id=1, replica_groups=mesh['prow'=4,'pcol'=8] {'pcol'}, dimensions={1}, use_global_device_ids=true | all-gather | bytes 589824 | tf_op jit(solution)/shard_map/all_gather | solution.py:60
  76.6 0.6 fusion.14
  77.3 1.0 negate_multiply_fusion.1
  78.3 1.1 convolution_add_fusion
  79.5 0.4 convolution_bitcast_fusion.1
  80.0 0.4 convolution_bitcast_fusion
  80.4 0.8 pad_maximum_fusion
  81.2 32.0 %all-reduce.7.cloned.1.call-done = f32[256,256]{1,0:T(8,128)} async-done(((f32[256,256]{1,0:T(8,128)}), f32[256,256]{1,0:T(8,128)}) %all-reduce.7.cloned.1.call-update) | async-done | bytes 262160 | tf_op jit(solution)/shard_map/psum | solution.py:25
  113.2 1.0 negate_multiply_fusion
  114.2 1.1 fusion.4
  115.3 0.6 constant_dynamic-slice_fusion
  116.0 132.6 %all-reduce.9.cloned.1.call-done = (f32[2,256,256]{2,1,0:T(8,128)}, f32[256,256]{1,0:T(8,128)}) async-done(((f32[2,256,256]{2,1,0:T(8,128)}, f32[256,256]{1,0:T(8,128)}), (f32[2,256,256]{2,1,0:T(8,128)}, f32[256,256]{1,0:T(8,128)})) %all-reduce.9.cloned.1.call-update) | async-done | bytes 786448 | tf_op jit(solution)/shard_map/psum | solution.py:31
  248.6 1.1 fusion.1
  249.7 0.6 fusion
  250.3 0.6 constant_dynamic-slice_fusion.1
  250.9 0.1 dynamic-slice_bitcast_fusion
  251.0 0.6 fusion.15
  251.6 0.7 copy.14
  252.3 1.5 dynamic-slice_subtract_fusion
  (30 shorter events, 0.7 us)
Async XLA Ops:
  7.2 34.3 %copy-start = (f32[512,256]{1,0:T(8,128)S(1)}, f32[512,256]{1,0:T(8,128)}, u32[]{:S(2)}) copy-start(f32[512,256]{1,0:T(8,128)} %param.8) | copy-start | bytes 1572868
  7.2 70.1 %all-reduce.5.cloned.1.call-start = ((), (), s32[]{:S(2)}) async-start(), calls=%async_computation | async-start | bytes 524288 | tf_op jit(solution)/shard_map/psum | solution.py:25
  7.2 0.7 copy-start.6
  7.2 0.7 copy-start.7
  42.7 2.6 %copy-start.5 = (f32[512,32]{0,1:T(8,128)S(1)}, f32[512,32]{0,1:T(8,128)}, u32[]{:S(2)}) copy-start(f32[512,32]{0,1:T(8,128)} %param.10) | copy-start | bytes 196612
  42.8 70.5 %all-reduce.7.cloned.1.call-start = ((), (), s32[]{:S(2)}) async-start(), calls=%async_computation.1 | async-start | bytes 524288 | tf_op jit(solution)/shard_map/psum | solution.py:25
  77.2 1.1 copy-start.1
  78.3 1.1 copy-start.4
  79.5 169.1 %all-reduce.9.cloned.1.call-start = ((), (), s32[]{:S(2)}) async-start(), calls=%async_computation.2 | async-start | bytes 1572864 | tf_op jit(solution)/shard_map/psum | solution.py:31
  115.3 133.3 %copy-start.3 = (f32[256,256]{1,0:T(8,128)S(1)}, f32[256,256]{1,0:T(8,128)}, u32[]{:S(2)}) copy-start(f32[256,256]{1,0:T(8,128)} %param.12) | copy-start | bytes 786436
  248.6 1.1 copy-start.2
Sparse Core Ops, SparseCore 0:
  42.9 33.3 all-reduce.4
  79.6 33.5 all-reduce.6
  118.5 130.0 all-reduce.8
where the time goes:
time: 261 us; the launch traced here: 260 us
  waiting for transfers between devices  165 us (63%)
  blocking collectives  64.4 us (25%)
  between operations  15.2 us (6%)
  matrix products  6.15 us (2%)
  other arithmetic  5.56 us (2%)
  local copies, waits for them, and re-layouts  4.23 us (2%)
    psum x1, waiting for transfers between devices, total_terms(): return lax.psum(stacked, ('prow', 'pcol'))  133 us
    all_gather x1, blocking collectives, on_device(): lax.all_gather(panel_parent, 'pcol', axis=1, tiled=True)  33.2 us
    psum x2, waiting for transfers between devices, row_total(): total = lax.psum(partial_value, 'prow')  32 us
    all_gather x1, blocking collectives, on_device(): lax.all_gather(panel_child, 'pcol', axis=1, tiled=True)  31.2 us
  transfers between devices with their start and end apart: 3, of which 2 were waited for; matrix products, arithmetic and copies ran while one was open for 2% of the time, Pallas kernels for 0%

commit v1 on v0

--- a/solution.py
+++ b/solution.py
@@ -28,7 +28,7 @@
 
 
 def total_terms(stacked):
-    return lax.psum(stacked, ("prow", "pcol"))
+    return lax.psum(lax.psum(stacked, "pcol"), "prow")
 
 
 def column_terms(row_part, blocks):

time: 261 us -> 241 us (0.923)
  waiting for transfers between devices: 165 us -> 145 us
    psum x1 -> x2, waiting for transfers between devices: 133 us -> 112 us  [total_terms(): return lax.psum(lax.psum(stacked, 'pcol'), 'prow')]
  transfers between devices with their start and end apart: 3 -> 4, of which waited for: 2 -> 3; matrix products, arithmetic and copies ran while one was open for 2% -> 2% of each run, Pallas kernels for 0% -> 0%
where the time goes in v1:
time: 241 us; the launch traced here: 240 us
  waiting for transfers between devices  145 us (60%)
  blocking collectives  64.4 us (27%)
  between operations  15.2 us (6%)
  matrix products  6.16 us (3%)
  other arithmetic  5.56 us (2%)
  local copies, waits for them, and re-layouts  4.23 us (2%)
    psum x2, waiting for transfers between devices, total_terms(): return lax.psum(lax.psum(stacked, 'pcol'), 'prow')  112 us
    all_gather x1, blocking collectives, on_device(): lax.all_gather(panel_parent, 'pcol', axis=1, tiled=True)  33.2 us
    psum x2, waiting for transfers between devices, row_total(): total = lax.psum(partial_value, 'prow')  32 us
    all_gather x1, blocking collectives, on_device(): lax.all_gather(panel_child, 'pcol', axis=1, tiled=True)  31.2 us
  transfers between devices with their start and end apart: 4, of which 3 were waited for; matrix products, arithmetic and copies ran while one was open for 2% of the time, Pallas kernels for 0%

profile of v1, /device:TPU:0, one launch (start us, length us, event | category | flops | bytes accessed | tf_op | source)
XLA Modules:
  0.0 240.4 jit_solution(14519205985333883006)
XLA Ops:
  7.3 0.7 copy-done.6
  8.1 33.2 %all_gather.6 = f32[512,256]{0,1:T(8,128)S(1)} all-gather(f32[512,32]{0,1:T(8,128)} %param.9), channel_id=1, replica_groups=mesh['prow'=4,'pcol'=8] {'pcol'}, dimensions={1}, use_global_device_ids=true | all-gather | bytes 589824 | tf_op jit(solution)/shard_map/all_gather | solution.py:59
  41.4 1.3 fusion.12
  42.8 0.6 dynamic_slice.45
  43.4 0.6 dynamic_slice.37
  45.4 31.2 %all_gather.7 = f32[512,256]{0,1:T(8,128)S(1)} all-gather(f32[512,32]{0,1:T(8,128)S(1)} %copy-done.5), channel_id=1, replica_groups=mesh['prow'=4,'pcol'=8] {'pcol'}, dimensions={1}, use_global_device_ids=true | all-gather | bytes 589824 | tf_op jit(solution)/shard_map/all_gather | solution.py:60
  76.6 0.6 fusion.13
  77.3 1.0 negate_multiply_fusion.1
  78.3 1.1 convolution_add_fusion
  79.5 0.4 convolution_bitcast_fusion.2
  80.0 0.4 convolution_bitcast_fusion.1
  80.4 0.8 pad_maximum_fusion
  81.2 32.0 %all-reduce.9.cloned.1.call-done = f32[256,256]{1,0:T(8,128)} async-done(((f32[256,256]{1,0:T(8,128)}), f32[256,256]{1,0:T(8,128)}) %all-reduce.9.cloned.1.call-update) | async-done | bytes 262160 | tf_op jit(solution)/shard_map/psum | solution.py:25
  113.2 1.0 negate_multiply_fusion
  114.2 1.1 convolution_bitcast_fusion
  115.4 76.6 %all-reduce.11.cloned.1.call-done = (f32[2,256,256]{2,1,0:T(8,128)}, f32[1,256,256]{2,1,0:T(8,128)}) async-done(((f32[2,256,256]{2,1,0:T(8,128)}, f32[1,256,256]{2,1,0:T(8,128)}), (f32[2,256,256]{2,1,0:T(8,128)}, f32[1,256,256]{2,1,0:T(8,128)})) %all-reduce.11.cloned.1.call-update) | async-done | bytes 786448 | tf_op jit(solution)/shard_map/psum | solution.py:31
  192.1 0.6 constant_dynamic-slice_fusion
  192.7 35.8 %all-reduce.13.cloned.1.call-done = (f32[2,256,256]{2,1,0:T(8,128)}, f32[256,256]{1,0:T(8,128)}) async-done(((f32[2,256,256]{2,1,0:T(8,128)}, f32[256,256]{1,0:T(8,128)}), (f32[2,256,256]{2,1,0:T(8,128)}, f32[256,256]{1,0:T(8,128)})) %all-reduce.13.cloned.1.call-update) | async-done | bytes 786448 | tf_op jit(solution)/shard_map/psum | solution.py:31
  228.5 1.1 fusion.1
  229.7 0.6 fusion
  230.3 0.6 constant_dynamic-slice_fusion.1
  231.0 0.6 fusion.14
  231.6 0.7 copy.14
  232.3 1.5 dynamic-slice_subtract_fusion
  (33 shorter events, 0.8 us)
Async XLA Ops:
  7.2 34.3 %copy-start = (f32[512,256]{1,0:T(8,128)S(1)}, f32[512,256]{1,0:T(8,128)}, u32[]{:S(2)}) copy-start(f32[512,256]{1,0:T(8,128)} %param.8) | copy-start | bytes 1572868
  7.2 70.1 %all-reduce.7.cloned.1.call-start = ((), (), s32[]{:S(2)}) async-start(), calls=%async_computation | async-start | bytes 524288 | tf_op jit(solution)/shard_map/psum | solution.py:25
  7.2 0.7 copy-start.6
  7.2 0.7 copy-start.7
  42.7 2.6 %copy-start.5 = (f32[512,32]{0,1:T(8,128)S(1)}, f32[512,32]{0,1:T(8,128)}, u32[]{:S(2)}) copy-start(f32[512,32]{0,1:T(8,128)} %param.10) | copy-start | bytes 196612
  42.8 70.5 %all-reduce.9.cloned.1.call-start = ((), (), s32[]{:S(2)}) async-start(), calls=%async_computation.1 | async-start | bytes 524288 | tf_op jit(solution)/shard_map/psum | solution.py:25
  77.3 1.1 copy-start.1
  78.3 1.1 copy-start.4
  79.5 112.5 %all-reduce.11.cloned.1.call-start = ((), (), s32[]{:S(2)}) async-start(), calls=%async_computation.2 | async-start | bytes 1572864 | tf_op jit(solution)/shard_map/psum | solution.py:31
  115.3 113.2 %all-reduce.13.cloned.1.call-start = ((), (), s32[]{:S(2)}) async-start(), calls=%async_computation.3 | async-start | bytes 1572864 | tf_op jit(solution)/shard_map/psum | solution.py:31
  192.0 36.5 %copy-start.3 = (f32[256,256]{1,0:T(8,128)S(1)}, f32[256,256]{1,0:T(8,128)}, u32[]{:S(2)}) copy-start(f32[256,256]{1,0:T(8,128)} %param.12) | copy-start | bytes 786436
  228.5 1.1 copy-start.2
Sparse Core Ops, SparseCore 0:
  42.9 33.3 all-reduce.6
  79.6 33.5 all-reduce.8
  116.8 75.2 all-reduce.10
  194.4 34.1 all-reduce.12
